TPU v7x, 32 devices: a whole 2x2x4 slice. The times are simulated.
32 devices in a mesh: dp: 8 (over y, x, core), rep: 4 (over z).
Axes of the slice: x: 2, y: 2, z: 4, core: 2. Of those that a mesh axis runs over, the one named last changes fastest.
Arguments:
- tokens: bfloat16 [4096, 2048], P(('dp', 'rep')), may hold values from -6 to 6
- cotangent: bfloat16 [4096, 2048], P(('dp', 'rep')), may hold values from -0.125 to 0.125
- doc_ids: int32 [64, 64], P(('dp', 'rep')), may hold values from 0 to 3, never falling along the last dimension, each value on 1 to 32 neighbouring positions
- valid_len: int32 [64], P(('dp', 'rep')), may hold values from 16 to 64
- w_qkv: bfloat16 [2048, 384], P('dp'), may hold values from -0.125 to 0.125
- w_out: bfloat16 [2048, 128], P('dp'), may hold values from -0.5 to 0.5
- norm_gain: bfloat16 [2048], P('dp'), may hold values from 0.5 to 1.5
Outputs:
- grad_qkv: float32 [2048, 384], P('dp')
- grad_out: float32 [2048, 128], P('dp')
- grad_gain: float32 [2048], P('dp')
Inputs may be any that keep to these rules, and one draw needn't show every extreme that they name: `doc_ids`: within each row of 64 positions the ids never fall, and a document has 1 to 32 positions.
All inputs are finite; a program needn't handle non-finite values.
Results may differ from a plain program's by a relative error of at most 0.0079.
Values may be sent and summed in bfloat16 or wider, within the bound.
A program may use at most 64 MiB of HBM per device.

v0:
```python
import math
import jax
import jax.numpy as jnp
from jax import lax
from jax.sharding import PartitionSpec as P

NORM_EPS = 1e-06
ROPE_BASE = 1000000.0


def rotate(vector):
    half_size = vector.shape[-1] // 2
    return jnp.concatenate([-vector[..., half_size:], vector[..., :half_size]], axis=-1)


def unrotate(vector):
    half_size = vector.shape[-1] // 2
    return jnp.concatenate([vector[..., half_size:], -vector[..., :half_size]], axis=-1)


def tables(doc_rows, head_size):
    seq_length = doc_rows.shape[1]
    earlier = jnp.sum((doc_rows[:, None, :] < doc_rows[:, :, None]).astype(jnp.int32), axis=2)
    offsets = (jnp.arange(seq_length, dtype=jnp.int32)[None, :] - earlier).astype(jnp.float32)
    frequency = ROPE_BASE ** (-2.0 * jnp.arange(head_size // 2, dtype=jnp.float32) / head_size)
    angles = offsets[:, :, None] * frequency
    angles = jnp.concatenate([angles, angles], axis=2)
    return (jnp.cos(angles), jnp.sin(angles))


def forward_pass(inputs, doc_rows, w_qkv_full, gain_full):
    batches, seq_length, model_width = inputs.shape
    head_size = w_qkv_full.shape[1] // 3
    scale = 1.0 / math.sqrt(head_size)
    wide_in = inputs.astype(jnp.float32)
    inverse_rms = lax.rsqrt(jnp.mean(wide_in * wide_in, axis=2, keepdims=True) + NORM_EPS)
    scaled_in = wide_in * inverse_rms
    normed = (scaled_in * gain_full.astype(jnp.float32)).astype(jnp.bfloat16)
    projected = jnp.dot(
        normed.reshape(-1, model_width), w_qkv_full, preferred_element_type=jnp.float32
    )
    projected = projected.reshape(batches, seq_length, 3 * head_size)
    cosine, sine_part = tables(doc_rows, head_size)
    queries = projected[:, :, :head_size]
    keys_raw = projected[:, :, head_size : 2 * head_size]
    values_raw = projected[:, :, 2 * head_size :]
    query_rot = ((queries * cosine + rotate(queries) * sine_part) * scale).astype(jnp.bfloat16)
    key_rot = (keys_raw * cosine + rotate(keys_raw) * sine_part).astype(jnp.bfloat16)
    values = values_raw.astype(jnp.bfloat16)
    scores = jnp.einsum("msh,mth->mst", query_rot, key_rot, preferred_element_type=jnp.float32)
    order_row = jnp.arange(seq_length, dtype=jnp.int32)[:, None]
    order_col = jnp.arange(seq_length, dtype=jnp.int32)[None, :]
    allowed = (doc_rows[:, :, None] == doc_rows[:, None, :]) & (order_col <= order_row)[None]
    raised = jnp.where(allowed, jnp.exp(scores), 0.0)
    probabilities = raised / jnp.sum(raised, axis=2, keepdims=True)
    probs_low = probabilities.astype(jnp.bfloat16)
    attended = jnp.einsum(
        "mst,mth->msh", probs_low, values, preferred_element_type=jnp.float32
    ).astype(jnp.bfloat16)
    return (
        scaled_in,
        normed,
        query_rot,
        key_rot,
        values,
        probabilities,
        probs_low,
        attended,
        cosine,
        sine_part,
    )


def backward_pass(saved, live_dy, w_qkv_full, w_out_full):
    (
        scaled_in,
        normed,
        query_rot,
        key_rot,
        values,
        probabilities,
        probs_low,
        attended,
        cosine,
        sine_part,
    ) = saved
    batches, seq_length, model_width = live_dy.shape
    head_size = w_out_full.shape[1]
    scale = 1.0 / math.sqrt(head_size)
    d_attended = jnp.dot(
        live_dy.reshape(-1, model_width), w_out_full, preferred_element_type=jnp.float32
    )
    d_attended = d_attended.reshape(batches, seq_length, head_size).astype(jnp.bfloat16)
    d_probs = jnp.einsum("msh,mth->mst", d_attended, values, preferred_element_type=jnp.float32)
    d_values = jnp.einsum("mst,msh->mth", probs_low, d_attended, preferred_element_type=jnp.float32)
    d_scores = (
        probabilities * (d_probs - jnp.sum(probabilities * d_probs, axis=2, keepdims=True))
    ).astype(jnp.bfloat16)
    d_query = (
        jnp.einsum("mst,mth->msh", d_scores, key_rot, preferred_element_type=jnp.float32) * scale
    )
    d_key = jnp.einsum("mst,msh->mth", d_scores, query_rot, preferred_element_type=jnp.float32)
    d_query = d_query * cosine + unrotate(d_query * sine_part)
    d_key = d_key * cosine + unrotate(d_key * sine_part)
    d_qkv = jnp.concatenate([d_query, d_key, d_values], axis=2).astype(jnp.bfloat16)
    d_normed = lax.dot_general(
        d_qkv.reshape(-1, 3 * head_size),
        w_qkv_full,
        (((1,), (1,)), ((), ())),
        preferred_element_type=jnp.float32,
    )
    gain_term = jnp.sum(d_normed * scaled_in.reshape(-1, model_width), axis=0)
    return (d_qkv, gain_term)


def shards(tokens, cotangent, doc_ids, valid_len, w_qkv, w_out, norm_gain):
    batches, seq_length = doc_ids.shape
    model_width = tokens.shape[1]
    inputs = tokens.reshape(batches, seq_length, model_width)
    live_rows = jnp.arange(seq_length, dtype=jnp.int32)[None, :] < valid_len[:, None]
    live_dy = jnp.where(
        live_rows[:, :, None],
        cotangent.reshape(batches, seq_length, model_width),
        jnp.zeros((), jnp.bfloat16),
    )
    full_set = (
        lax.all_gather(w_qkv, "dp", axis=0, tiled=True),
        lax.all_gather(w_out, "dp", axis=0, tiled=True),
        lax.all_gather(norm_gain, "dp", axis=0, tiled=True),
    )
    saved = forward_pass(inputs, doc_ids, full_set[0], full_set[2])
    qkv_all, gain_total = backward_pass(saved, live_dy, full_set[0], full_set[1])
    normed_all = saved[1]
    attended_all = saved[7]
    head_size = w_out.shape[1]
    normed_flat = normed_all.reshape(-1, model_width)
    qkv_flat = qkv_all.reshape(-1, 3 * head_size)
    attended_flat = attended_all.reshape(-1, head_size)
    grad_qkv = lax.dot_general(
        normed_flat, qkv_flat, (((0,), (0,)), ((), ())), preferred_element_type=jnp.float32
    )
    grad_out = lax.dot_general(
        live_dy.reshape(-1, model_width),
        attended_flat,
        (((0,), (0,)), ((), ())),
        preferred_element_type=jnp.float32,
    )
    shares = (
        lax.psum_scatter(grad_qkv, "dp", scatter_dimension=0, tiled=True),
        lax.psum_scatter(grad_out, "dp", scatter_dimension=0, tiled=True),
    )
    shares = lax.psum((shares[0], shares[1]), "rep")
    gain_whole = lax.psum(gain_total, ("dp", "rep"))
    owned_rows = w_qkv.shape[0]
    gain_start = lax.axis_index("dp") * owned_rows
    gain_owned = lax.dynamic_slice_in_dim(gain_whole, gain_start, owned_rows, 0)
    replicas = lax.axis_size("rep")
    return (shares[0] / replicas, shares[1] / replicas, gain_owned / replicas)


def solution(mesh):
    in_specs = (
        P(("dp", "rep"), None),
        P(("dp", "rep"), None),
        P(("dp", "rep"), None),
        P(("dp", "rep")),
        P("dp", None),
        P("dp", None),
        P("dp"),
    )
    out_specs = (P("dp", None), P("dp", None), P("dp"))
    return jax.shard_map(shards, mesh=mesh, in_specs=in_specs, out_specs=out_specs, check_vma=False)
```

profile of v0, /device:TPU:0, one launch (start us, length us, event | category | flops | bytes accessed | tf_op | source)
XLA Modules:
  0.0 179.0 jit_solution(12147938299542766601)
XLA Ops:
  7.2 0.7 all-gather.3.cloned.1.call-update
  8.0 0.7 iota_compare_fusion.1
  8.8 1.3 multiply_reduce_fusion
  10.2 0.7 reshape.109
  10.8 10.4 %all-gather = bf16[8,1,256]{2,1,0:T(2,128)(2,1)S(1)} all-gather(bf16[1,1,256]{2,1,0:T(2,128)(2,1)S(1)} %reshape.109), channel_id=1, replica_groups=mesh['dp'=8,'rep'=4] {'dp'}, dimensions={0}, use_global_device_ids=true | all-gather | bytes 4608 | tf_op jit(solution)/shard_map/all_gather | solution.py:129
  21.3 0.8 convert_reduce_fusion
  22.1 9.8 %all_gather.11 = bf16[2048,128]{1,0:T(8,128)(2,1)S(1)} all-gather(bf16[256,128]{1,0:T(8,128)(2,1)} %param.12), channel_id=1, replica_groups=mesh['dp'=8,'rep'=4] {'dp'}, dimensions={0}, use_global_device_ids=true | all-gather | bytes 589824 | tf_op jit(solution)/shard_map/all_gather | solution.py:128
  32.2 0.3 convolution_convert_fusion.2
  32.7 5.5 %all-gather.3.cloned.1.call-done = bf16[2048,384]{1,0:T(8,128)(2,1)} async-done(((bf16[256,384]{1,0:T(8,128)(2,1)}), bf16[2048,384]{1,0:T(8,128)(2,1)}) %all-gather.3.cloned.1.call-update) | async-done | bytes 1572880 | tf_op jit(solution)/shard_map/all_gather | solution.py:127
  38.2 1.9 %fusion = f32[2,64,384]{2,1,0:T(8,128)S(1)} fusion(bf16[2,64,2048]{2,1,0:T(8,128)(2,1)S(1)} %bitcast.33, bf16[2048,384]{1,0:T(8,128)(2,1)} %all-gather.3.cloned.1.call-done), kind=kOutput, calls=%fused_computation.3 | convolution fusion | flops 201326592 | bytes 2293760 | tf_op jit(solution)/shard_map/dot_general | solution.py:39
  40.3 0.3 fusion.21
  40.8 1.5 convolution_bitcast_fusion.1
  42.4 0.3 fusion.32
  42.8 0.3 fusion.25
  43.3 0.3 fusion.26
  43.7 2.3 %convolution_bitcast_fusion = f32[2048,384]{1,0:T(8,128)} fusion(f32[2048]{0:T(1024)S(1)} %bitcast.38, f32[2,64]{1,0:T(2,128)S(1)} %rsqrt.13, bf16[2,64,128]{2,1,0:T(8,128)(2,1)S(1)} %convolution_convert_fusion.1, bf16[2,64,128]{2,1,0:T(8,128)(2,1)S(1)} %fusion.26, bf16[2,64,128]{2,1,0:T(8,128)(2,1)S(1)} %get-tuple-element.11, ...), kind=kOutput, calls=%fused_computation | convolution fusion | flops 202670080 | bytes 3777024 | tf_op jit(solution)/shard_map/dot_general | solution.py:139
  46.1 32.4 %reduce-scatter.5.cloned.1.call-done = f32[256,128]{1,0:T(8,128)} async-done(((f32[2048,128]{1,0:T(8,128)}), f32[256,128]{1,0:T(8,128)}) %reduce-scatter.5.cloned.1.call-update) | async-done | bytes 131088 | tf_op jit(solution)/shard_map/reduce_scatter | solution.py:150
  78.5 49.5 %reduce-scatter.3.cloned.1.call-done = f32[256,384]{1,0:T(8,128)} async-done(((f32[2048,384]{1,0:T(8,128)}), f32[256,384]{1,0:T(8,128)}) %reduce-scatter.3.cloned.1.call-update) | async-done | bytes 393232 | tf_op jit(solution)/shard_map/reduce_scatter | solution.py:149
  128.0 0.6 fusion.2
  128.7 39.5 %psum.23 = f32[2048]{0:T(1024)S(1)} all-reduce(f32[2048]{0:T(1024)S(1)} %fusion.2), channel_id=1, replica_groups=mesh['dp'=8,'rep'=4] {'dp','rep'}, use_global_device_ids=true, to_apply=%region_9.10 | all-reduce | flops 2048 | bytes 16384 | tf_op jit(solution)/shard_map/psum | solution.py:153
  168.2 0.6 dynamic-slice_multiply_fusion
  168.8 0.4 all-reduce.3.cloned.1.call-done
  169.2 1.8 broadcast_multiply_fusion
  170.9 1.6 broadcast_multiply_fusion.1
  (32 shorter events, 1.5 us)
Async XLA Ops:
  7.2 24.9 %copy-start.1 = (bf16[128,2048]{1,0:T(8,128)(2,1)S(1)}, bf16[128,2048]{1,0:T(8,128)(2,1)}, u32[]{:S(2)}) copy-start(bf16[128,2048]{1,0:T(8,128)(2,1)} %param.8) | copy-start | bytes 1572868
  7.2 31.0 %all-gather.3.cloned.1.call-start = ((), (), s32[]{:S(2)}) async-start(), calls=%async_computation.2 | async-start | bytes 1769472 | tf_op jit(solution)/shard_map/all_gather | solution.py:127
  7.9 70.6 %reduce-scatter.5.cloned.1.call-start = ((), (), s32[]{:S(2)}) async-start(), calls=%async_computation.4 | async-start | bytes 1179648 | tf_op jit(solution)/shard_map/reduce_scatter | solution.py:150
  8.8 23.7 %copy-start = (bf16[128,2048]{1,0:T(8,128)(2,1)S(1)}, bf16[128,2048]{1,0:T(8,128)(2,1)}, u32[]{:S(2)}) copy-start(bf16[128,2048]{1,0:T(8,128)(2,1)} %param.7) | copy-start | bytes 1572868
  38.2 2.5 %copy-start.3 = (s32[2,64]{1,0:T(2,128)S(1)}, s32[2,64]{1,0:T(2,128)}, u32[]{:S(2)}) copy-start(s32[2,64]{1,0:T(2,128)} %param.9) | copy-start | bytes 1540
  42.4 85.6 %reduce-scatter.3.cloned.1.call-start = ((), (), s32[]{:S(2)}) async-start(), calls=%async_computation.3 | async-start | bytes 3538944 | tf_op jit(solution)/shard_map/reduce_scatter | solution.py:149
  46.0 82.0 %copy-start.2 = (bf16[2048,384]{1,0:T(8,128)(2,1)S(1)}, bf16[2048,384]{1,0:T(8,128)(2,1)}, u32[]{:S(2)}) copy-start(bf16[2048,384]{1,0:T(8,128)(2,1)} %all-gather.3.cloned.1.call-done) | copy-start | bytes 4718596
  46.1 123.1 %all-reduce.3.cloned.1.call-start = ((), (), s32[]{:S(2)}) async-start(), calls=%async_computation.5 | async-start | bytes 1048576 | tf_op jit(solution)/shard_map/psum | solution.py:152
Sparse Core Ops, SparseCore 0:
  9.9 28.2 all-gather.2
  42.5 35.9 reduce-scatter.4
  81.9 46.0 reduce-scatter.2
  130.3 38.8 all-reduce.2
where the time goes:
time: 179 us
  waiting for transfers between devices  88.5 us (49%)
  blocking collectives  59.7 us (33%)
  between operations  13.9 us (8%)
  other arithmetic  8.19 us (5%)
  matrix products  7.7 us (4%)
    reduce_scatter x1, waiting for transfers between devices, shards(): lax.psum_scatter(grad_qkv, 'dp', scatter_dimension=0, tiled=True)  49.5 us
    psum x1, blocking collectives, shards(): gain_whole = lax.psum(gain_total, ('dp', 'rep'))  39.5 us
    reduce_scatter x1, waiting for transfers between devices, shards(): lax.psum_scatter(grad_out, 'dp', scatter_dimension=0, tiled=True)  32.4 us
    all_gather x1, blocking collectives, shards(): lax.all_gather(norm_gain, 'dp', axis=0, tiled=True)  10.4 us
    all_gather x1, blocking collectives, shards(): lax.all_gather(w_out, 'dp', axis=0, tiled=True)  9.83 us
    all_gather x1, waiting for transfers between devices, shards(): lax.all_gather(w_qkv, 'dp', axis=0, tiled=True)  5.52 us
    div x3, other arithmetic, shards(): return (shares[0] / replicas, shares[1] / replicas, gain_owned / replicas)  3.97 us
  transfers between devices with their start and end apart: 4, of which 4 were waited for; matrix products, arithmetic and copies ran while one was open for 5% of the time, Pallas kernels for 0%

commit v1 on v0

--- a/solution.py
+++ b/solution.py
@@ -6,6 +6,27 @@
 
 NORM_EPS = 1e-06
 ROPE_BASE = 1000000.0
+
+
+def ring_gather(shard, axis, dim):
+    size, index, extent = (lax.axis_size(axis), lax.axis_index(axis), shard.shape[dim])
+    right = [(i, (i + 1) % size) for i in range(size)]
+    downward = [(i, (i - 1) % size) for i in range(size)]
+    out = jnp.zeros((*shard.shape[:dim], size * extent, *shard.shape[dim + 1 :]), shard.dtype)
+    out = lax.dynamic_update_slice_in_dim(out, shard, index * extent, axis=dim)
+    from_left = from_right = shard
+    half = size // 2
+    for step in range(1, half + 1):
+        from_left = lax.ppermute(from_left, axis, right)
+        out = lax.dynamic_update_slice_in_dim(
+            out, from_left, (index - step) % size * extent, axis=dim
+        )
+        if step < size - half:
+            from_right = lax.ppermute(from_right, axis, downward)
+            out = lax.dynamic_update_slice_in_dim(
+                out, from_right, (index + step) % size * extent, axis=dim
+            )
+    return out
 
 
 def rotate(vector):
@@ -125,7 +146,7 @@
     )
     full_set = (
         lax.all_gather(w_qkv, "dp", axis=0, tiled=True),
-        lax.all_gather(w_out, "dp", axis=0, tiled=True),
+        ring_gather(w_out, "dp", 0),
         lax.all_gather(norm_gain, "dp", axis=0, tiled=True),
     )
     saved = forward_pass(inputs, doc_ids, full_set[0], full_set[2])

time: 179 us -> 182 us (1.017)
  blocking collectives: 59.7 us -> 49.2 us
  starting transfers between devices: 0.16 us -> 8.99 us
  waiting for transfers between devices: 88.5 us -> 91.9 us
    ppermute x0 -> x7, waiting for transfers between devices: none -> 10.2 us  [the longest x4 10.2 us: ring_gather(): from_left = lax.ppermute(from_left, axis, right)]
    all_gather x1 -> x0, blocking collectives: 9.83 us -> none  [shards(): lax.all_gather(w_out, 'dp', axis=0, tiled=True)]
    ppermute x0 -> x7, starting transfers between devices: none -> 8.83 us  [the longest x3 7.88 us: ring_gather(): from_right = lax.ppermute(from_right, axis, downward)]
    all_gather x1, waiting for transfers between devices: 5.52 us -> 0.02 us  [shards(): lax.all_gather(w_qkv, 'dp', axis=0, tiled=True)]
  transfers between devices with their start and end apart: 4 -> 11, of which waited for: 4 -> 6; matrix products, arithmetic and copies ran while one was open for 5% -> 6% of each run, Pallas kernels for 0% -> 0%
where the time goes in v1:
time: 182 us
  waiting for transfers between devices  91.9 us (50%)
  blocking collectives  49.2 us (27%)
  between operations  14.1 us (8%)
  starting transfers between devices  8.99 us (5%)
  other arithmetic  8.12 us (4%)
  matrix products  7.68 us (4%)
  local copies, waits for them, and re-layouts  1.9 us (1%)
    reduce_scatter x1, waiting for transfers between devices, shards(): lax.psum_scatter(grad_qkv, 'dp', scatter_dimension=0, tiled=True)  49.5 us
    psum x1, blocking collectives, shards(): gain_whole = lax.psum(gain_total, ('dp', 'rep'))  39.6 us
    reduce_scatter x1, waiting for transfers between devices, shards(): lax.psum_scatter(grad_out, 'dp', scatter_dimension=0, tiled=True)  31.8 us
    ppermute x4, waiting for transfers between devices, ring_gather(): from_left = lax.ppermute(from_left, axis, right)  10.2 us
    all_gather x1, blocking collectives, shards(): lax.all_gather(norm_gain, 'dp', axis=0, tiled=True)  9.62 us
    ppermute x3, starting transfers between devices, ring_gather(): from_right = lax.ppermute(from_right, axis, downward)  7.88 us
    div x3, other arithmetic, shards(): return (shares[0] / replicas, shares[1] / replicas, gain_owned / replicas)  3.97 us
  transfers between devices with their start and end apart: 11, of which 6 were waited for; matrix products, arithmetic and copies ran while one was open for 6% of the time, Pallas kernels for 0%

profile of v1, /device:TPU:0, one launch (start us, length us, event | category | flops | bytes accessed | tf_op | source)
XLA Modules:
  0.0 181.9 jit_solution(16544490035922999297)
XLA Ops:
  7.2 0.5 collective-permute-start
  7.8 2.9 %collective-permute-start.1 = (bf16[256,128]{1,0:T(8,128)(2,1)}, bf16[256,128]{1,0:T(8,128)(2,1)S(1)}, u32[]{:S(2)}, u32[]{:S(2)}) collective-permute-start(bf16[256,128]{1,0:T(8,128)(2,1)} %param.12), channel_id=1, source_target_pairs={{0,28},{4,0},{8,4},{12,8},{16,12},{20,16},{24,20},{28,24},{1,29},{... | collective-permute-start | bytes 196616 | tf_op jit(solution)/shard_map/ppermute | solution.py:25
  10.9 0.7 iota_compare_fusion.1
  11.7 1.2 multiply_reduce_fusion
  13.0 0.7 reshape.109
  13.6 9.6 %all-gather = bf16[8,1,256]{2,1,0:T(2,128)(2,1)S(1)} all-gather(bf16[1,1,256]{2,1,0:T(2,128)(2,1)S(1)} %reshape.109), channel_id=1, replica_groups=mesh['dp'=8,'rep'=4] {'dp'}, dimensions={0}, use_global_device_ids=true | all-gather | bytes 4608 | tf_op jit(solution)/shard_map/all_gather | solution.py:150
  23.3 0.8 convert_reduce_fusion
  24.3 0.9 constant_dynamic-update-slice_fusion.7
  25.6 0.4 collective-permute-start.2
  26.0 2.3 %collective-permute-start.3 = (bf16[256,128]{1,0:T(8,128)(2,1)S(1)}, bf16[256,128]{1,0:T(8,128)(2,1)S(1)}, u32[]{:S(2)}, u32[]{:S(2)}) collective-permute-start(bf16[256,128]{1,0:T(8,128)(2,1)S(1)} %collective-permute-done.1), channel_id=1, source_target_pairs={{0,28},{4,0},{8,4},{12,8},{16,12},{20,16},{24,20},{28,24},{1,29},{... | collective-permute-start | bytes 196616 | tf_op jit(solution)/shard_map/ppermute | solution.py:25
  28.3 1.9 %collective-permute-done.2 = bf16[256,128]{1,0:T(8,128)(2,1)S(1)} collective-permute-done((bf16[256,128]{1,0:T(8,128)(2,1)S(1)}, bf16[256,128]{1,0:T(8,128)(2,1)S(1)}, u32[]{:S(2)}, u32[]{:S(2)}) %collective-permute-start.2) | collective-permute-done | bytes 65568 | tf_op jit(solution)/shard_map/ppermute | solution.py:20
  30.2 2.6 %collective-permute-start.5 = (bf16[256,128]{1,0:T(8,128)(2,1)S(1)}, bf16[256,128]{1,0:T(8,128)(2,1)S(1)}, u32[]{:S(2)}, u32[]{:S(2)}) collective-permute-start(bf16[256,128]{1,0:T(8,128)(2,1)S(1)} %collective-permute-done.3), channel_id=1, source_target_pairs={{0,28},{4,0},{8,4},{12,8},{16,12},{20,16},{24,20},{28,24},{1,29},{... | collective-permute-start | bytes 196616 | tf_op jit(solution)/shard_map/ppermute | solution.py:25
  32.9 3.8 %collective-permute-done.4 = bf16[256,128]{1,0:T(8,128)(2,1)S(1)} collective-permute-done((bf16[256,128]{1,0:T(8,128)(2,1)S(1)}, bf16[256,128]{1,0:T(8,128)(2,1)S(1)}, u32[]{:S(2)}, u32[]{:S(2)}) %collective-permute-start.4) | collective-permute-done | bytes 65568 | tf_op jit(solution)/shard_map/ppermute | solution.py:20
  36.7 4.5 %collective-permute-done.6 = bf16[256,128]{1,0:T(8,128)(2,1)S(1)} collective-permute-done((bf16[256,128]{1,0:T(8,128)(2,1)S(1)}, bf16[256,128]{1,0:T(8,128)(2,1)S(1)}, u32[]{:S(2)}, u32[]{:S(2)}) %collective-permute-start.6) | collective-permute-done | bytes 65568 | tf_op jit(solution)/shard_map/ppermute | solution.py:20
  41.6 1.8 %fusion = f32[2,64,384]{2,1,0:T(8,128)S(1)} fusion(bf16[2,64,2048]{2,1,0:T(8,128)(2,1)S(1)} %bitcast.33, bf16[2048,384]{1,0:T(8,128)(2,1)} %all-gather.3.cloned.1.call-done), kind=kOutput, calls=%fused_computation.3 | convolution fusion | flops 201326592 | bytes 2293760 | tf_op jit(solution)/shard_map/dot_general | solution.py:60
  44.3 1.5 convolution_bitcast_fusion.1
  47.1 2.3 %convolution_bitcast_fusion = f32[2048,384]{1,0:T(8,128)} fusion(f32[2048]{0:T(1024)S(1)} %bitcast.38, f32[2,64]{1,0:T(2,128)S(1)} %rsqrt.13, bf16[2,64,128]{2,1,0:T(8,128)(2,1)S(1)} %convolution_convert_fusion.1, bf16[2,64,128]{2,1,0:T(8,128)(2,1)S(1)} %fusion.26, bf16[2,64,128]{2,1,0:T(8,128)(2,1)S(1)} %get-tuple-element.11, ...), kind=kOutput, calls=%fused_computation | convolution fusion | flops 202670080 | bytes 3777024 | tf_op jit(solution)/shard_map/dot_general | solution.py:160
  49.5 31.8 %reduce-scatter.5.cloned.1.call-done = f32[256,128]{1,0:T(8,128)} async-done(((f32[2048,128]{1,0:T(8,128)}), f32[256,128]{1,0:T(8,128)}) %reduce-scatter.5.cloned.1.call-update) | async-done | bytes 131088 | tf_op jit(solution)/shard_map/reduce_scatter | solution.py:171
  81.4 49.5 %reduce-scatter.3.cloned.1.call-done = f32[256,384]{1,0:T(8,128)} async-done(((f32[2048,384]{1,0:T(8,128)}), f32[256,384]{1,0:T(8,128)}) %reduce-scatter.3.cloned.1.call-update) | async-done | bytes 393232 | tf_op jit(solution)/shard_map/reduce_scatter | solution.py:170
  130.9 0.6 fusion.2
  131.5 39.6 %psum.23 = f32[2048]{0:T(1024)S(1)} all-reduce(f32[2048]{0:T(1024)S(1)} %fusion.2), channel_id=1, replica_groups=mesh['dp'=8,'rep'=4] {'dp','rep'}, use_global_device_ids=true, to_apply=%region_9.10 | all-reduce | flops 2048 | bytes 16384 | tf_op jit(solution)/shard_map/psum | solution.py:174
  171.1 0.6 dynamic-slice_multiply_fusion
  172.0 1.8 broadcast_multiply_fusion
  173.8 1.6 broadcast_multiply_fusion.1
  (54 shorter events, 3.7 us)
Async XLA Ops:
  7.2 18.2 %copy-start = (bf16[128,2048]{1,0:T(8,128)(2,1)S(1)}, bf16[128,2048]{1,0:T(8,128)(2,1)}, u32[]{:S(2)}) copy-start(bf16[128,2048]{1,0:T(8,128)(2,1)} %param.7) | copy-start | bytes 1572868
  7.2 18.1 %copy-start.1 = (bf16[128,2048]{1,0:T(8,128)(2,1)S(1)}, bf16[128,2048]{1,0:T(8,128)(2,1)}, u32[]{:S(2)}) copy-start(bf16[128,2048]{1,0:T(8,128)(2,1)} %param.8) | copy-start | bytes 1572868
  7.2 34.4 %all-gather.3.cloned.1.call-start = ((), (), s32[]{:S(2)}) async-start(), calls=%async_computation.2 | async-start | bytes 1769472 | tf_op jit(solution)/shard_map/all_gather | solution.py:148
  7.2 18.4 %collective-permute-start = (bf16[256,128]{1,0:T(8,128)(2,1)}, bf16[256,128]{1,0:T(8,128)(2,1)S(1)}, u32[]{:S(2)}, u32[]{:S(2)}) collective-permute-start(bf16[256,128]{1,0:T(8,128)(2,1)} %param.12), channel_id=1, source_target_pairs={{0,4},{4,8},{8,12},{12,16},{16,20},{20,24},{24,28},{28,0},{1,5},{5... | collective-permute-start | bytes 196616 | tf_op jit(solution)/shard_map/ppermute | solution.py:20
  7.8 18.2 %collective-permute-start.1 = (bf16[256,128]{1,0:T(8,128)(2,1)}, bf16[256,128]{1,0:T(8,128)(2,1)S(1)}, u32[]{:S(2)}, u32[]{:S(2)}) collective-permute-start(bf16[256,128]{1,0:T(8,128)(2,1)} %param.12), channel_id=1, source_target_pairs={{0,28},{4,0},{8,4},{12,8},{16,12},{20,16},{24,20},{28,24},{1,29},{... | collective-permute-start | bytes 196616 | tf_op jit(solution)/shard_map/ppermute | solution.py:25
  10.7 70.6 %reduce-scatter.5.cloned.1.call-start = ((), (), s32[]{:S(2)}) async-start(), calls=%async_computation.4 | async-start | bytes 1179648 | tf_op jit(solution)/shard_map/reduce_scatter | solution.py:171
  25.6 4.6 %collective-permute-start.2 = (bf16[256,128]{1,0:T(8,128)(2,1)S(1)}, bf16[256,128]{1,0:T(8,128)(2,1)S(1)}, u32[]{:S(2)}, u32[]{:S(2)}) collective-permute-start(bf16[256,128]{1,0:T(8,128)(2,1)S(1)} %collective-permute-done), channel_id=1, source_target_pairs={{0,4},{4,8},{8,12},{12,16},{16,20},{20,24},{24,28},{28,0},{1,5},{5... | collective-permute-start | bytes 196616 | tf_op jit(solution)/shard_map/ppermute | solution.py:20
  26.0 4.2 %collective-permute-start.3 = (bf16[256,128]{1,0:T(8,128)(2,1)S(1)}, bf16[256,128]{1,0:T(8,128)(2,1)S(1)}, u32[]{:S(2)}, u32[]{:S(2)}) collective-permute-start(bf16[256,128]{1,0:T(8,128)(2,1)S(1)} %collective-permute-done.1), channel_id=1, source_target_pairs={{0,28},{4,0},{8,4},{12,8},{16,12},{20,16},{24,20},{28,24},{1,29},{... | collective-permute-start | bytes 196616 | tf_op jit(solution)/shard_map/ppermute | solution.py:25
  30.2 6.5 %collective-permute-start.4 = (bf16[256,128]{1,0:T(8,128)(2,1)S(1)}, bf16[256,128]{1,0:T(8,128)(2,1)S(1)}, u32[]{:S(2)}, u32[]{:S(2)}) collective-permute-start(bf16[256,128]{1,0:T(8,128)(2,1)S(1)} %collective-permute-done.2), channel_id=1, source_target_pairs={{0,4},{4,8},{8,12},{12,16},{16,20},{20,24},{24,28},{28,0},{1,5},{5... | collective-permute-start | bytes 196616 | tf_op jit(solution)/shard_map/ppermute | solution.py:20
  30.2 6.5 %collective-permute-start.5 = (bf16[256,128]{1,0:T(8,128)(2,1)S(1)}, bf16[256,128]{1,0:T(8,128)(2,1)S(1)}, u32[]{:S(2)}, u32[]{:S(2)}) collective-permute-start(bf16[256,128]{1,0:T(8,128)(2,1)S(1)} %collective-permute-done.3), channel_id=1, source_target_pairs={{0,28},{4,0},{8,4},{12,8},{16,12},{20,16},{24,20},{28,24},{1,29},{... | collective-permute-start | bytes 196616 | tf_op jit(solution)/shard_map/ppermute | solution.py:25
  36.7 4.6 %collective-permute-start.6 = (bf16[256,128]{1,0:T(8,128)(2,1)S(1)}, bf16[256,128]{1,0:T(8,128)(2,1)S(1)}, u32[]{:S(2)}, u32[]{:S(2)}) collective-permute-start(bf16[256,128]{1,0:T(8,128)(2,1)S(1)} %collective-permute-done.4), channel_id=1, source_target_pairs={{0,4},{4,8},{8,12},{12,16},{16,20},{20,24},{24,28},{28,0},{1,5},{5... | collective-permute-start | bytes 196616 | tf_op jit(solution)/shard_map/ppermute | solution.py:20
  41.6 2.5 %copy-start.3 = (s32[2,64]{1,0:T(2,128)S(1)}, s32[2,64]{1,0:T(2,128)}, u32[]{:S(2)}) copy-start(s32[2,64]{1,0:T(2,128)} %param.9) | copy-start | bytes 1540
  45.8 85.1 %reduce-scatter.3.cloned.1.call-start = ((), (), s32[]{:S(2)}) async-start(), calls=%async_computation.3 | async-start | bytes 3538944 | tf_op jit(solution)/shard_map/reduce_scatter | solution.py:170
  49.5 81.4 %copy-start.2 = (bf16[2048,384]{1,0:T(8,128)(2,1)S(1)}, bf16[2048,384]{1,0:T(8,128)(2,1)}, u32[]{:S(2)}) copy-start(bf16[2048,384]{1,0:T(8,128)(2,1)} %all-gather.3.cloned.1.call-done) | copy-start | bytes 4718596
  49.5 122.6 %all-reduce.3.cloned.1.call-start = ((), (), s32[]{:S(2)}) async-start(), calls=%async_computation.5 | async-start | bytes 1048576 | tf_op jit(solution)/shard_map/psum | solution.py:173
Sparse Core Ops, SparseCore 0:
  10.9 28.6 all-gather.2
  45.9 35.4 reduce-scatter.4
  84.8 46.0 reduce-scatter.2
  133.1 38.8 all-reduce.2
